TPU v7x, 32 devices: a whole 2x2x4 slice. The times are simulated.
32 devices in a mesh: rep: 16 (over z, y, core), fsdp: 2 (over x).
Axes of the slice: x: 2, y: 2, z: 4, core: 2. Of those that a mesh axis runs over, the one named last changes fastest.
Arguments:
- activations: bfloat16 [4096, 8192], P(('rep', 'fsdp')), may hold values from -7.75 to 7.75
- upstream: bfloat16 [4096, 512], P(('rep', 'fsdp')), may hold values from -0.484375 to 0.484375
- q_start: float32 [2, 4, 512], P('fsdp'), may hold values from -6 to 6
Outputs:
- error_feedback: bfloat16 [16, 8192, 512], P('rep', 'fsdp')
- p_basis: float32 [2, 4, 4096], P('fsdp')
- q_factor: float32 [2, 4, 512], P('fsdp')
All inputs are finite; a program needn't handle non-finite values.
Results may differ from a plain program's by a relative error of at most 0.015.
Values may be sent and summed in bfloat16 or wider, within the bound.
A program may use at most 64 MiB of HBM per device.

v0:
```python
import jax
import jax.numpy as jnp
from jax import lax
from jax.sharding import PartitionSpec as P


def contract_tokens(left, right):
    return lax.dot_general(
        left, right, (((0,), (0,)), ((), ())), preferred_element_type=jnp.float32
    )


def rounded(term):
    short = lax.optimization_barrier(term.astype(jnp.bfloat16))
    return short.astype(jnp.float32)


def on_device(activations, upstream, q_start):
    high = lax.Precision.HIGHEST
    groups = lax.axis_size("fsdp")
    replicas = lax.axis_size("rep")
    tok_rows = activations.shape[0]
    shard_rows = activations.shape[1] // groups
    columns = lax.all_to_all(activations, "fsdp", split_axis=1, concat_axis=0, tiled=True)
    cotangent_all = lax.all_gather(upstream, "fsdp", axis=0, tiled=True)
    shard = jnp.zeros((shard_rows, upstream.shape[1]), jnp.float32)
    for source in range(groups):
        left = columns[source * tok_rows : (source + 1) * tok_rows]
        right = cotangent_all[source * tok_rows : (source + 1) * tok_rows]
        shard = shard + rounded(contract_tokens(left, right))
    q_local = q_start[0]
    left_local = lax.dot_general(
        q_local, shard, (((1,), (1,)), ((), ())), precision=high, preferred_element_type=jnp.float32
    )
    p_sum = lax.psum(left_local, "rep")
    basis = []
    for i in range(p_sum.shape[0]):
        vector = p_sum[i]
        for earlier in basis:
            vector = vector - jnp.sum(vector * earlier) * earlier
        basis.append(vector / jnp.sqrt(jnp.sum(vector * vector) + 1e-06))
    p_basis = jnp.stack(basis)
    right_local = jnp.dot(p_basis, shard, precision=high)
    q_factor = lax.psum(right_local, "rep")
    approx = lax.dot_general(
        p_basis,
        q_factor / replicas,
        (((0,), (0,)), ((), ())),
        precision=high,
        preferred_element_type=jnp.float32,
    )
    error_feedback = (shard - approx).astype(jnp.bfloat16)
    return (error_feedback[None], p_basis[None], q_factor[None])


def solution(mesh):
    in_specs = (P(("rep", "fsdp"), None), P(("rep", "fsdp"), None), P("fsdp", None, None))
    out_specs = (P("rep", "fsdp", None), P("fsdp", None, None), P("fsdp", None, None))
    return jax.shard_map(
        on_device, mesh=mesh, in_specs=in_specs, out_specs=out_specs, check_vma=False
    )
```

profile of v0, /device:TPU:0, one launch (start us, length us, event | category | flops | bytes accessed | tf_op | source)
XLA Modules:
  0.0 222.7 jit_solution(16569028851342070702)
XLA Ops:
  7.2 0.0 copy-start
  7.2 0.0 copy-start.3
  7.2 4.1 %copy.6 = bf16[128,8192]{0,1:T(8,128)(2,1)} copy(bf16[128,8192]{1,0:T(8,128)(2,1)} %param.3) | data formatting | bytes 4194304 | tf_op args[0]
  11.3 4.2 %all-to-all-start = ((bf16[128,2,4096]{0,2,1:T(8,128)(2,1)}), bf16[128,2,4096]{0,2,1:T(8,128)(2,1)S(1)}, u32[]{:S(2)}, u32[]{:S(2)}) async-start(bf16[128,2,4096]{0,2,1:T(8,128)(2,1)} %bitcast.26), calls=%async_computation | async-start | bytes 4194304 | tf_op jit(solution)/shard_map/all_to_all | solution.py:24
  15.5 0.0 all-reduce.2.cloned.1.call-start
  15.5 0.0 copy-done.3
  15.5 28.7 %all_gather.3 = bf16[256,512]{1,0:T(8,128)(2,1)S(1)} all-gather(bf16[128,512]{1,0:T(8,128)(2,1)S(1)} %copy-done.3), channel_id=1, replica_groups=mesh['rep'=16,'fsdp'=2] {'fsdp'}, dimensions={0}, use_global_device_ids=true | all-gather | bytes 393216 | tf_op jit(solution)/shard_map/all_gather | solution.py:25
  44.2 0.0 all-to-all-done
  44.2 1.2 convolution_convert_fusion
  45.4 0.0 copy-start.1
  45.5 1.2 convolution_convert_fusion.1
  46.7 0.8 copy-done.1
  47.5 1.9 copy-done.2
  49.4 0.0 copy-done
  49.4 8.4 %fusion.3 = f32[4,4096]{1,0:T(4,128)} fusion(bf16[4096,512]{1,0:T(8,128)(2,1)S(1)} %convolution_convert_fusion, bf16[4096,512]{1,0:T(8,128)(2,1)S(1)} %convolution_convert_fusion.1, f32[1,4,512]{2,1,0:T(4,128)S(1)} %copy-done), kind=kOutput, calls=%fused_computation.7 | convolution fusion | flops 106954752 | bytes 8462336 | tf_op jit(solution)/shard_map/dot_general | solution.py:32
  57.8 0.0 all-reduce.2.cloned.1.call-update
  57.9 87.0 %all-reduce.2.cloned.1.call-done = f32[4,4096]{1,0:T(4,128)} async-done(((f32[4,4096]{1,0:T(4,128)}), f32[4,4096]{1,0:T(4,128)}) %all-reduce.2.cloned.1.call-update) | async-done | bytes 65552 | tf_op jit(solution)/shard_map/psum | solution.py:35
  144.8 1.5 multiply_reduce_fusion.9
  147.0 1.1 fusion.11
  148.1 0.6 multiply_reduce_fusion.8
  148.7 1.3 multiply_reduce_fusion.3
  150.7 2.5 %multiply_reduce_fusion.2 = (f32[]{:T(128)}, f32[]{:T(128)}, f32[4096]{0:T(1024)S(1)}) fusion(f32[4096]{0:T(1024)S(1)} %bitcast.36, f32[4096]{0:T(1024)S(1)} %bitcast.29, f32[]{:T(128)} %get-tuple-element.5, f32[4096]{0:T(1024)S(1)} %bitcast.39, f32[]{:T(128)} %get-tuple-element.6, f32[]{:T(128)S(6)} %sqrt.13, f32[4096]{0:T(1024)S(1)} %bitcast.34, ...), kind=kLoop, calls=%fused_computation.17 | loop fusion | flops 45054 | bytes 81944 | tf_op jit(solution)/shard_map/reduce_sum | solution.py:40
  153.2 1.8 multiply_reduce_fusion.4
  155.7 1.9 multiply_reduce_fusion.1
  157.6 1.3 multiply_reduce_fusion
  159.5 4.8 %subtract_divide_fusion = (f32[1,4096]{1,0:T(1,128)S(1)}, f32[1,4096]{1,0:T(1,128)S(1)}, f32[1,4096]{1,0:T(1,128)S(1)}) fusion(f32[1,4096]{1,0:T(1,128)S(1)} %get-tuple-element.17, f32[]{:T(128)S(6)} %sqrt.15, f32[]{:T(128)} %get-tuple-element.11, f32[]{:T(128)} %get-tuple-element.3, f32[]{:T(128)} %get-tuple-element.5, ...), kind=kLoop, calls=%fused_computation.14 | loop fusion | flops 61440 | bytes 114724 | tf_op jit(solution)/shard_map/div | solution.py:41
  164.3 7.1 %fusion = f32[4,512]{1,0:T(4,128)S(1)} fusion(bf16[4096,512]{1,0:T(8,128)(2,1)} %copy-done.1, bf16[4096,512]{1,0:T(8,128)(2,1)} %copy-done.2, f32[1,4096]{1,0:T(1,128)S(1)} %get-tuple-element.8, f32[1,4096]{1,0:T(1,128)S(1)} %get-tuple-element.9, f32[1,4096]{1,0:T(1,128)S(1)} %get-tuple-element.10, f32[1,4096]{1,0:T(1,128)S(1)} %get-tuple-element.17), kind=kOutput, calls=%fused_computation.2 | convolution fusion | flops 107003904 | bytes 8462336 | tf_op jit(solution)/shard_map/dot_general | solution.py:43
  171.4 0.7 fusion.10
  172.1 32.4 %psum.15 = f32[4,512]{1,0:T(4,128)S(1)} all-reduce(f32[4,512]{1,0:T(4,128)S(1)} %fusion), channel_id=1, replica_groups=mesh['rep'=16,'fsdp'=2] {'rep'}, use_global_device_ids=true, to_apply=%region_11.0 | all-reduce | flops 2048 | bytes 16384 | tf_op jit(solution)/shard_map/psum | solution.py:44
  204.6 0.0 copy-start.4
  204.6 11.3 %fusion.2 = bf16[1,4096,512]{2,1,0:T(8,128)(2,1)} fusion(bf16[4096,512]{1,0:T(8,128)(2,1)} %copy-done.1, bf16[4096,512]{1,0:T(8,128)(2,1)} %copy-done.2, f32[4,512]{1,0:T(4,128)S(1)} %psum.15, f32[1,4096]{1,0:T(1,128)S(1)} %get-tuple-element.8, f32[1,4096]{1,0:T(1,128)S(1)} %get-tuple-element.9, f32[1,4096]{1,0:T(1,128)S(1)} %get-tuple-element.10, ...), kind=kOutput, calls=%fused_computation.6 | convolution fusion | flops 111200256 | bytes 12656640 | tf_op jit(solution)/shard_map/dot_general | solution.py:45
  215.9 0.0 copy-done.4
  (1 shorter events, 0.0 us)
Async XLA Ops:
  7.2 42.2 %copy-start = (f32[1,4,512]{2,1,0:T(4,128)S(1)}, f32[1,4,512]{2,1,0:T(4,128)}, u32[]{:S(2)}) copy-start(f32[1,4,512]{2,1,0:T(4,128)} %param.5) | copy-start | bytes 24580
  7.2 8.4 %copy-start.3 = (bf16[128,512]{1,0:T(8,128)(2,1)S(1)}, bf16[128,512]{1,0:T(8,128)(2,1)}, u32[]{:S(2)}) copy-start(bf16[128,512]{1,0:T(8,128)(2,1)} %param.4) | copy-start | bytes 393220
  11.3 32.9 %all-to-all-start = ((bf16[128,2,4096]{0,2,1:T(8,128)(2,1)}), bf16[128,2,4096]{0,2,1:T(8,128)(2,1)S(1)}, u32[]{:S(2)}, u32[]{:S(2)}) async-start(bf16[128,2,4096]{0,2,1:T(8,128)(2,1)} %bitcast.26), calls=%async_computation | async-start | bytes 4194304 | tf_op jit(solution)/shard_map/all_to_all | solution.py:24
  15.5 129.3 %all-reduce.2.cloned.1.call-start = ((), (), s32[]{:S(2)}) async-start(), calls=%async_computation.1 | async-start | bytes 131072 | tf_op jit(solution)/shard_map/psum | solution.py:35
  45.4 2.0 copy-start.1
  47.5 1.9 copy-start.2
  204.6 11.3 %copy-start.4 = (f32[4,512]{1,0:T(4,128)}, f32[4,512]{1,0:T(4,128)S(1)}, u32[]{:S(2)}) copy-start(f32[4,512]{1,0:T(4,128)S(1)} %psum.15) | copy-start | bytes 24580
Sparse Core Ops, SparseCore 0:
  58.0 86.7 all-reduce.1
where the time goes:
time: 223 us
  waiting for transfers between devices  87 us (39%)
  blocking collectives  61.1 us (27%)
  matrix products  29.3 us (13%)
  other arithmetic  17.4 us (8%)
  between operations  16.8 us (8%)
  local copies, waits for them, and re-layouts  6.82 us (3%)
  starting transfers between devices  4.24 us (2%)
    psum x1, waiting for transfers between devices, on_device(): p_sum = lax.psum(left_local, 'rep')  87 us
    psum x1, blocking collectives, on_device(): q_factor = lax.psum(right_local, 'rep')  32.4 us
    all_gather x1, blocking collectives, on_device(): cotangent_all = lax.all_gather(upstream, 'fsdp', axis=0, tiled=True)  28.7 us
    dot_general x1, matrix products, on_device(): lax.dot_general(p_basis, q_factor / replicas, (((0,), (0,)), ((), ())), p...  11.3 us
    dot_general x1, matrix products, on_device(): lax.dot_general(q_local, shard, (((1,), (1,)), ((), ())), precision=high,...  8.44 us
    dot_general x1, matrix products, on_device(): right_local = jnp.dot(p_basis, shard, precision=high)  7.14 us
    unnamed x11, local copies, waits for them, and re-layouts  6.82 us
    reduce_sum x4, other arithmetic, on_device(): vector = vector - jnp.sum(vector * earlier) * earlier  6.39 us
  transfers between devices with their start and end apart: 2, of which 1 were waited for; matrix products, arithmetic and copies ran while one was open for 0% of the time, Pallas kernels for 0%

commit v1 on v0

--- a/solution.py
+++ b/solution.py
@@ -2,6 +2,11 @@
 import jax.numpy as jnp
 from jax import lax
 from jax.sharding import PartitionSpec as P
+
+
+def add_all(x, name):
+    blocks = lax.all_gather(x, name)
+    return jnp.sum(blocks, axis=0)
 
 
 def contract_tokens(left, right):
@@ -41,7 +46,7 @@
         basis.append(vector / jnp.sqrt(jnp.sum(vector * vector) + 1e-06))
     p_basis = jnp.stack(basis)
     right_local = jnp.dot(p_basis, shard, precision=high)
-    q_factor = lax.psum(right_local, "rep")
+    q_factor = add_all(right_local, "rep")
     approx = lax.dot_general(
         p_basis,
         q_factor / replicas,

time: 223 us -> 213 us (0.955)
  blocking collectives: 61.1 us -> 51.1 us
    psum x1 -> x0, blocking collectives: 32.4 us -> none  [on_device(): q_factor = lax.psum(right_local, 'rep')]
    all_gather x0 -> x1, blocking collectives: none -> 22.4 us  [add_all(): blocks = lax.all_gather(x, name)]
where the time goes in v1:
time: 213 us
  waiting for transfers between devices  87 us (41%)
  blocking collectives  51.1 us (24%)
  matrix products  29.3 us (14%)
  other arithmetic  17.5 us (8%)
  between operations  16.8 us (8%)
  local copies, waits for them, and re-layouts  6.81 us (3%)
  starting transfers between devices  4.24 us (2%)
    psum x1, waiting for transfers between devices, on_device(): p_sum = lax.psum(left_local, 'rep')  87 us
    all_gather x1, blocking collectives, on_device(): cotangent_all = lax.all_gather(upstream, 'fsdp', axis=0, tiled=True)  28.7 us
    all_gather x1, blocking collectives, add_all(): blocks = lax.all_gather(x, name)  22.4 us
    dot_general x1, matrix products, on_device(): lax.dot_general(p_basis, q_factor / replicas, (((0,), (0,)), ((), ())), p...  11.3 us
    dot_general x1, matrix products, on_device(): lax.dot_general(q_local, shard, (((1,), (1,)), ((), ())), precision=high,...  8.44 us
    dot_general x1, matrix products, on_device(): right_local = jnp.dot(p_basis, shard, precision=high)  7.14 us
    unnamed x11, local copies, waits for them, and re-layouts  6.81 us
    reduce_sum x4, other arithmetic, on_device(): vector = vector - jnp.sum(vector * earlier) * earlier  6.39 us
  transfers between devices with their start and end apart: 2, of which 1 were waited for; matrix products, arithmetic and copies ran while one was open for 0% of the time, Pallas kernels for 0%

profile of v1, /device:TPU:0, one launch (start us, length us, event | category | flops | bytes accessed | tf_op | source)
XLA Modules:
  0.0 212.8 jit_solution(2980421579178745298)
XLA Ops:
  7.2 0.0 copy-start
  7.2 0.0 copy-start.3
  7.2 4.1 %copy.9 = bf16[128,8192]{0,1:T(8,128)(2,1)} copy(bf16[128,8192]{1,0:T(8,128)(2,1)} %param.3) | data formatting | bytes 4194304 | tf_op args[0]
  11.3 4.2 %all-to-all-start = ((bf16[128,2,4096]{0,2,1:T(8,128)(2,1)}), bf16[128,2,4096]{0,2,1:T(8,128)(2,1)S(1)}, u32[]{:S(2)}, u32[]{:S(2)}) async-start(bf16[128,2,4096]{0,2,1:T(8,128)(2,1)} %bitcast.28), calls=%async_computation | async-start | bytes 4194304 | tf_op jit(solution)/shard_map/all_to_all | solution.py:29
  15.5 0.0 all-reduce.2.cloned.1.call-start
  15.5 0.0 copy-done.3
  15.5 28.7 %all_gather.9 = bf16[256,512]{1,0:T(8,128)(2,1)S(1)} all-gather(bf16[128,512]{1,0:T(8,128)(2,1)S(1)} %copy-done.3), channel_id=1, replica_groups=mesh['rep'=16,'fsdp'=2] {'fsdp'}, dimensions={0}, use_global_device_ids=true | all-gather | bytes 393216 | tf_op jit(solution)/shard_map/all_gather | solution.py:30
  44.2 0.0 all-to-all-done
  44.2 1.2 convolution_convert_fusion
  45.4 0.0 copy-start.1
  45.5 1.2 convolution_convert_fusion.1
  46.7 0.8 copy-done.1
  47.5 0.0 copy-start.2
  47.5 1.9 copy-done.2
  49.4 0.0 copy-done
  49.4 8.4 %fusion.3 = f32[4,4096]{1,0:T(4,128)} fusion(bf16[4096,512]{1,0:T(8,128)(2,1)S(1)} %convolution_convert_fusion, bf16[4096,512]{1,0:T(8,128)(2,1)S(1)} %convolution_convert_fusion.1, f32[1,4,512]{2,1,0:T(4,128)S(1)} %copy-done), kind=kOutput, calls=%fused_computation.7 | convolution fusion | flops 106954752 | bytes 8462336 | tf_op jit(solution)/shard_map/dot_general | solution.py:37
  57.8 0.0 all-reduce.2.cloned.1.call-update
  57.9 87.0 %all-reduce.2.cloned.1.call-done = f32[4,4096]{1,0:T(4,128)} async-done(((f32[4,4096]{1,0:T(4,128)}), f32[4,4096]{1,0:T(4,128)}) %all-reduce.2.cloned.1.call-update) | async-done | bytes 65552 | tf_op jit(solution)/shard_map/psum | solution.py:40
  144.8 1.5 multiply_reduce_fusion.9
  147.0 1.1 fusion.12
  148.1 0.6 multiply_reduce_fusion.8
  148.7 1.3 multiply_reduce_fusion.3
  150.7 2.5 %multiply_reduce_fusion.2 = (f32[]{:T(128)}, f32[]{:T(128)}, f32[4096]{0:T(1024)S(1)}) fusion(f32[4096]{0:T(1024)S(1)} %bitcast.38, f32[4096]{0:T(1024)S(1)} %bitcast.31, f32[]{:T(128)} %get-tuple-element.5, f32[4096]{0:T(1024)S(1)} %bitcast.41, f32[]{:T(128)} %get-tuple-element.6, f32[]{:T(128)S(6)} %sqrt.13, f32[4096]{0:T(1024)S(1)} %bitcast.36, ...), kind=kLoop, calls=%fused_computation.18 | loop fusion | flops 45054 | bytes 81944 | tf_op jit(solution)/shard_map/reduce_sum | solution.py:45
  153.2 1.8 multiply_reduce_fusion.4
  155.7 1.9 multiply_reduce_fusion.1
  157.6 1.3 multiply_reduce_fusion
  159.5 4.8 %subtract_divide_fusion = (f32[1,4096]{1,0:T(1,128)S(1)}, f32[1,4096]{1,0:T(1,128)S(1)}, f32[1,4096]{1,0:T(1,128)S(1)}) fusion(f32[1,4096]{1,0:T(1,128)S(1)} %get-tuple-element.17, f32[]{:T(128)S(6)} %sqrt.15, f32[]{:T(128)} %get-tuple-element.11, f32[]{:T(128)} %get-tuple-element.3, f32[]{:T(128)} %get-tuple-element.5, ...), kind=kLoop, calls=%fused_computation.15 | loop fusion | flops 61440 | bytes 114724 | tf_op jit(solution)/shard_map/div | solution.py:46
  164.3 7.1 %fusion.4 = f32[1,4,512]{2,1,0:T(4,128)S(1)} fusion(bf16[4096,512]{1,0:T(8,128)(2,1)} %copy-done.1, bf16[4096,512]{1,0:T(8,128)(2,1)} %copy-done.2, f32[1,4096]{1,0:T(1,128)S(1)} %get-tuple-element.8, f32[1,4096]{1,0:T(1,128)S(1)} %get-tuple-element.9, f32[1,4096]{1,0:T(1,128)S(1)} %get-tuple-element.10, f32[1,4096]{1,0:T(1,128)S(1)} %get-tuple-element.17), kind=kOutput, calls=%fused_computation.8 | convolution fusion | flops 107003904 | bytes 8462336 | tf_op jit(solution)/shard_map/dot_general | solution.py:48
  171.4 0.7 fusion.11
  172.1 22.4 %all-gather.1 = f32[16,4,512]{2,1,0:T(4,128)S(1)} all-gather(f32[1,4,512]{2,1,0:T(4,128)S(1)} %fusion.4), channel_id=2, replica_groups=mesh['rep'=16,'fsdp'=2] {'rep'}, dimensions={0}, use_global_device_ids=true | all-gather | bytes 139264 | tf_op jit(solution)/shard_map/all_gather | solution.py:8
  194.6 11.3 %fusion.2 = bf16[1,4096,512]{2,1,0:T(8,128)(2,1)} fusion(bf16[4096,512]{1,0:T(8,128)(2,1)} %copy-done.1, bf16[4096,512]{1,0:T(8,128)(2,1)} %copy-done.2, f32[4,512]{1,0:T(4,128)S(1)} %reduce_sum.109, f32[1,4096]{1,0:T(1,128)S(1)} %get-tuple-element.8, f32[1,4096]{1,0:T(1,128)S(1)} %get-tuple-element.9, f32[1,4096]{1,0:T(1,128)S(1)} %get-tuple-element.10, ...), kind=kOutput, calls=%fused_computation.6 | convolution fusion | flops 111200256 | bytes 12656640 | tf_op jit(solution)/shard_map/dot_general | solution.py:50
  205.9 0.0 copy-done.4
  (2 shorter events, 0.0 us)
Async XLA Ops:
  7.2 42.2 %copy-start = (f32[1,4,512]{2,1,0:T(4,128)S(1)}, f32[1,4,512]{2,1,0:T(4,128)}, u32[]{:S(2)}) copy-start(f32[1,4,512]{2,1,0:T(4,128)} %param.5) | copy-start | bytes 24580
  7.2 8.4 %copy-start.3 = (bf16[128,512]{1,0:T(8,128)(2,1)S(1)}, bf16[128,512]{1,0:T(8,128)(2,1)}, u32[]{:S(2)}) copy-start(bf16[128,512]{1,0:T(8,128)(2,1)} %param.4) | copy-start | bytes 393220
  11.3 32.9 %all-to-all-start = ((bf16[128,2,4096]{0,2,1:T(8,128)(2,1)}), bf16[128,2,4096]{0,2,1:T(8,128)(2,1)S(1)}, u32[]{:S(2)}, u32[]{:S(2)}) async-start(bf16[128,2,4096]{0,2,1:T(8,128)(2,1)} %bitcast.28), calls=%async_computation | async-start | bytes 4194304 | tf_op jit(solution)/shard_map/all_to_all | solution.py:29
  15.5 129.3 %all-reduce.2.cloned.1.call-start = ((), (), s32[]{:S(2)}) async-start(), calls=%async_computation.1 | async-start | bytes 131072 | tf_op jit(solution)/shard_map/psum | solution.py:40
  45.4 2.0 copy-start.1
  47.5 1.9 copy-start.2
  194.6 11.3 %copy-start.4 = (f32[4,512]{1,0:T(4,128)}, f32[4,512]{1,0:T(4,128)S(1)}, u32[]{:S(2)}) copy-start(f32[4,512]{1,0:T(4,128)S(1)} %reduce_sum.109) | copy-start | bytes 24580
Sparse Core Ops, SparseCore 0:
  58.0 86.7 all-reduce.1
